TPU v7x, 32 devices: a whole 2x2x4 slice. The times are simulated.
32 devices in a mesh: gx: 4 (over y, x), gy: 8 (over z, core).
Axes of the slice: x: 2, y: 2, z: 4, core: 2. Of those that a mesh axis runs over, the one named last changes fastest.
Arguments:
- features: bfloat16 [64, 512, 128], P(('gx', 'gy')), may hold values from -11 to 11
- brick_pos: int32 [64], P(('gx', 'gy')), may hold values from 0 to 4, as said below
- cotangent: bfloat16 [64, 512, 128], P(('gx', 'gy')), may hold values from -40 to 40
- first_kernel: bfloat16 [27, 128, 128], replicated, may hold values from -0.109375 to 0.109375
- second_kernel: bfloat16 [27, 128, 128], replicated, may hold values from -0.109375 to 0.109375
- norm_gain: float32 [128], replicated, may hold values from 0.1 to 1.9
Outputs:
- block_out: bfloat16 [64, 512, 128], P(('gx', 'gy'))
- feature_grad: bfloat16 [64, 512, 128], P(('gx', 'gy'))
- kernel_update: float32 [2, 27, 128, 128], replicated
- gain_update: float32 [128], replicated
Inputs may be any that keep to these rules, and one draw needn't show every extreme that they name: `brick_pos`: on each device block the first k slots (k between max(1, 0) and 2, and k = 2 on at least one block) hold distinct positions below 4; the remaining slots hold 4.
All inputs are finite; a program needn't handle non-finite values.
Results may differ from a plain program's by a relative error of at most 0.0029.
Values may be sent and summed in bfloat16 or wider, within the bound.
No kernel may reach another device: no remote copies, remote signals or barrier semaphores. Data moves between devices by JAX's collectives and lax.ppermute only.
A program may use at most 128 MiB of HBM per device.

v0:
```python
import jax
import jax.numpy as jnp
from jax import lax
from jax.sharding import PartitionSpec as P

BX = 2
BY = 2
BZ = 1
POS = 4
clip_level = 0.5


def with_halo(cells, sides, width):
    for axis, dim in sides:
        count = lax.axis_size(axis)
        ends = count - 1
        head = lax.slice_in_dim(cells, 0, width, axis=dim)
        tail = lax.slice_in_dim(cells, cells.shape[dim] - width, cells.shape[dim], axis=dim)
        cells = jnp.concatenate(
            [
                lax.ppermute(tail, axis, [(i, (i + 1) % count) for i in range(ends)]),
                cells,
                lax.ppermute(head, axis, [((i + 1) % count, i) for i in range(ends)]),
            ],
            axis=dim,
        )
    return cells


def brick_coords(position):
    brick_x = position // (BY * BZ)
    brick_y = position // BZ % BY
    brick_z = position % BZ
    return (brick_x, brick_y, brick_z)


def activate(pre, norm_gain):
    average = jnp.mean(pre, axis=-1, keepdims=True)
    center = pre - average
    spread = jnp.mean(center * center, axis=-1, keepdims=True)
    normed = center * lax.rsqrt(spread + 1e-05) * norm_gain
    return normed * jax.nn.sigmoid(normed)


def apply_taps(tile_set, kernel, flipped):
    slot_count, channels = (tile_set.shape[0], tile_set.shape[-1])
    summed = jnp.zeros((slot_count * 512, channels), jnp.float32)
    for step_x in range(3):
        for step_y in range(3):
            for step_z in range(3):
                tap_index = (step_x * 3 + step_y) * 3 + step_z
                if flipped:
                    start_x, start_y, start_z = (2 - step_x, 2 - step_y, 2 - step_z)
                else:
                    start_x, start_y, start_z = (step_x, step_y, step_z)
                window = tile_set[
                    :, start_x : start_x + 8, start_y : start_y + 8, start_z : start_z + 8, :
                ]
                window = window.reshape(slot_count * 512, channels)
                if flipped:
                    summed = summed + lax.dot_general(
                        window,
                        kernel[tap_index],
                        (((1,), (1,)), ((), ())),
                        preferred_element_type=jnp.float32,
                    )
                else:
                    summed = summed + jnp.dot(
                        window, kernel[tap_index], preferred_element_type=jnp.float32
                    )
    return summed.reshape(slot_count, 512, channels)


def tap_grads(tile_set, upstream):
    slot_count, channels = (tile_set.shape[0], tile_set.shape[-1])
    flat_rows = upstream.reshape(slot_count * 512, channels)
    result = []
    for step_x in range(3):
        for step_y in range(3):
            for step_z in range(3):
                window = tile_set[
                    :, step_x : step_x + 8, step_y : step_y + 8, step_z : step_z + 8, :
                ]
                window = window.reshape(slot_count * 512, channels)
                result.append(
                    lax.dot_general(
                        window,
                        flat_rows,
                        (((0,), (0,)), ((), ())),
                        preferred_element_type=jnp.float32,
                    )
                )
    return jnp.stack(result)


def widen_grid(dense_grid):
    widened = with_halo(dense_grid, (("gx", 0), ("gy", 1)), 1)
    return jnp.pad(widened, ((0, 0), (0, 0), (1, 1), (0, 0)))


def clip_factor(squares, channels):
    entries = 54.0 * channels * channels + channels
    return jnp.minimum(1.0, clip_level / jnp.sqrt(squares / entries + 1e-06))


def per_device(features, brick_pos, cotangent, first_kernel, second_kernel, norm_gain):
    slot_count, channels = (features.shape[0], features.shape[2])
    is_live = brick_pos < POS
    brick_x, brick_y, brick_z = brick_coords(jnp.minimum(brick_pos, POS - 1))
    put_x = jnp.where(is_live, brick_x, BX)
    live_mask = is_live[:, None, None]
    given_rows = jnp.where(live_mask, features, jnp.zeros_like(features))
    upstream = jnp.where(live_mask, cotangent, jnp.zeros_like(cotangent))

    def tiles_for(values):
        bricks = jnp.zeros((BX, BY, BZ, 8, 8, 8, channels), values.dtype)
        bricks = bricks.at[put_x, brick_y, brick_z].set(
            values.reshape(slot_count, 8, 8, 8, channels), mode="drop"
        )
        dense_grid = bricks.transpose(0, 3, 1, 4, 2, 5, 6).reshape(BX * 8, BY * 8, BZ * 8, channels)
        padded = widen_grid(dense_grid)

        def take_tile(start_x, start_y, start_z):
            return lax.dynamic_slice(
                padded, (start_x * 8, start_y * 8, start_z * 8, start_x * 0), (10, 10, 10, channels)
            )

        return jax.vmap(take_tile)(brick_x, brick_y, brick_z)

    given_tiles = tiles_for(given_rows)
    first_pre = jnp.where(live_mask, apply_taps(given_tiles, first_kernel, False), 0.0)
    hidden_full, pullback = jax.vjp(activate, first_pre, norm_gain)
    hidden = jnp.where(live_mask, hidden_full, 0.0).astype(jnp.bfloat16)
    hidden_tiles = tiles_for(hidden)
    second_pre = jnp.where(live_mask, apply_taps(hidden_tiles, second_kernel, False), 0.0)
    block_out = (given_rows.astype(jnp.float32) + second_pre).astype(jnp.bfloat16)
    second_grad = tap_grads(hidden_tiles, upstream).reshape(-1)
    hidden_grad = jnp.where(live_mask, apply_taps(tiles_for(upstream), second_kernel, True), 0.0)
    pre_full, gain_grad = pullback(hidden_grad)
    pre_grad = jnp.where(live_mask, pre_full, 0.0).astype(jnp.bfloat16)
    first_grad = tap_grads(given_tiles, pre_grad).reshape(-1)
    back_conv = apply_taps(tiles_for(pre_grad), first_kernel, True)
    feature_grad = jnp.where(live_mask, upstream.astype(jnp.float32) + back_conv, 0.0).astype(
        jnp.bfloat16
    )
    combined, gain_summed = lax.psum(
        (jnp.concatenate([first_grad, second_grad]), gain_grad), ("gx", "gy")
    )
    shrink = clip_factor(
        jnp.sum(combined * combined) + jnp.sum(gain_summed * gain_summed), channels
    )
    updated = shrink * combined
    kernel_update = updated.reshape(2, 27, channels, channels)
    return (block_out, feature_grad, kernel_update, shrink * gain_summed)


def solution(mesh):
    in_specs = (
        P(("gx", "gy"), None, None),
        P(("gx", "gy")),
        P(("gx", "gy"), None, None),
        P(),
        P(),
        P(),
    )
    out_specs = (P(("gx", "gy"), None, None), P(("gx", "gy"), None, None), P(), P())
    return jax.shard_map(
        per_device, mesh=mesh, in_specs=in_specs, out_specs=out_specs, check_vma=False
    )
```

profile of v0, /device:TPU:0, one launch (start us, length us, event | category | flops | bytes accessed | tf_op | source)
XLA Modules:
  0.0 331.9 jit_solution(15290965411382618557)
XLA Ops:
  11.2 4.9 %collective-permute-start.8 = (bf16[1,16,8,128]{3,2,1,0:T(8,128)(2,1)S(1)}, bf16[1,16,8,128]{3,2,1,0:T(8,128)(2,1)S(1)}, u32[]{:S(2)}, u32[]{:S(2)}) collective-permute-start(bf16[1,16,8,128]{3,2,1,0:T(8,128)(2,1)S(1)} %get-tuple-element.24), channel_id=1, source_target_pairs={{0,8},{8,16},{16,24},{1,9},{9,17},{17,25},{2,10},{10,18},{18,26},{... | collective-permute-start | bytes 98312 | tf_op jit(solution)/shard_map/ppermute | solution.py:21
  18.3 4.5 %collective-permute-start = (bf16[1,16,8,128]{3,2,1,0:T(8,128)(2,1)S(1)}, bf16[1,16,8,128]{3,2,1,0:T(8,128)(2,1)S(1)}, u32[]{:S(2)}, u32[]{:S(2)}) collective-permute-start(bf16[1,16,8,128]{3,2,1,0:T(8,128)(2,1)S(1)} %get-tuple-element.28), channel_id=1, source_target_pairs={{0,8},{8,16},{16,24},{1,9},{9,17},{17,25},{2,10},{10,18},{18,26},{... | collective-permute-start | bytes 98312 | tf_op jit(solution)/shard_map/ppermute | solution.py:21
  22.8 1.3 collective-permute-start.1
  26.9 2.1 collective-permute-done.1
  29.0 2.7 collective-permute-start.2
  33.8 2.7 pad_slice_fusion.18
  36.6 1.4 fusion.300
  56.1 2.5 multiply_reduce_fusion.1
  58.8 2.7 fusion.293
  61.6 1.5 select_convert_fusion
  73.3 2.3 fusion.62
  76.5 4.9 %collective-permute-start.4 = (bf16[1,16,8,128]{3,2,1,0:T(8,128)(2,1)S(1)}, bf16[1,16,8,128]{3,2,1,0:T(8,128)(2,1)S(1)}, u32[]{:S(2)}, u32[]{:S(2)}) collective-permute-start(bf16[1,16,8,128]{3,2,1,0:T(8,128)(2,1)S(1)} %get-tuple-element.26), channel_id=1, source_target_pairs={{0,8},{8,16},{16,24},{1,9},{9,17},{17,25},{2,10},{10,18},{18,26},{... | collective-permute-start | bytes 98312 | tf_op jit(solution)/shard_map/ppermute | solution.py:21
  81.4 1.3 collective-permute-start.5
  82.7 45.0 %psum.15 = f32[128]{0:T(128)S(1)} all-reduce(f32[128]{0:T(128)S(1)} %copy-done.163), channel_id=1, replica_groups=mesh['gx'=4,'gy'=8] {'gx','gy'}, use_global_device_ids=true, to_apply=%region_11.12 | all-reduce | flops 128 | bytes 1024 | tf_op jit(solution)/shard_map/psum | solution.py:146
  131.0 4.2 %collective-permute-start.12 = (bf16[1,16,8,128]{3,2,1,0:T(8,128)(2,1)S(1)}, bf16[1,16,8,128]{3,2,1,0:T(8,128)(2,1)S(1)}, u32[]{:S(2)}, u32[]{:S(2)}) collective-permute-start(bf16[1,16,8,128]{3,2,1,0:T(8,128)(2,1)S(1)} %get-tuple-element.22), channel_id=1, source_target_pairs={{0,8},{8,16},{16,24},{1,9},{9,17},{17,25},{2,10},{10,18},{18,26},{... | collective-permute-start | bytes 98312 | tf_op jit(solution)/shard_map/ppermute | solution.py:21
  136.6 1.3 collective-permute-start.6
  137.9 1.3 collective-permute-start.7
  139.2 1.8 collective-permute-done.13
  141.7 3.5 %collective-permute-start.14 = (bf16[18,1,8,128]{3,2,1,0:T(8,128)(2,1)}, bf16[18,1,8,128]{3,2,1,0:T(8,128)(2,1)}, u32[]{:S(2)}, u32[]{:S(2)}) collective-permute-start(bf16[18,1,8,128]{3,2,1,0:T(8,128)(2,1)} %get-tuple-element.14), channel_id=1, source_target_pairs={{0,1},{1,2},{2,3},{3,4},{4,5},{5,6},{6,7},{8,9},{9,10},{10,11},{11... | collective-permute-start | bytes 110600 | tf_op jit(solution)/shard_map/ppermute | solution.py:21
  145.2 1.5 collective-permute-start.15
  147.7 1.8 gather_fusion.1
  149.5 2.7 pad_slice_fusion.36
  152.3 1.3 fusion.301
  153.6 1.8 pad_maximum_fusion.4
  155.3 1.8 gather_fusion.3
  157.2 2.7 pad_slice_fusion
  159.9 1.4 fusion.299
  170.3 2.0 pad_maximum_fusion
  172.3 1.4 convolution_add_fusion.77
  191.8 123.8 %all-reduce.6.cloned.1.call-done = f32[884736]{0:T(1024)} async-done(((f32[884736]{0:T(1024)}), f32[884736]{0:T(1024)}) %all-reduce.6.cloned.1.call-update) | async-done | bytes 3538960 | tf_op jit(solution)/shard_map/psum | solution.py:146
  315.6 3.5 %multiply_reduce_fusion = f32[]{:T(128)} fusion(f32[884736]{0:T(1024)} %all-reduce.6.cloned.1.call-done), kind=kLoop, calls=%fused_computation.9 | loop fusion | flops 1769471 | bytes 3538948 | tf_op jit(solution)/shard_map/reduce_sum | solution.py:150
  321.0 4.0 %broadcast_multiply_fusion = f32[884736]{0:T(1024)} fusion(f32[884736]{0:T(1024)} %all-reduce.6.cloned.1.call-done, f32[]{:T(128)S(6)} %min.7), kind=kLoop, calls=%fused_computation.82 | loop fusion | flops 884736 | bytes 7077892 | tf_op jit(solution)/shard_map/mul | solution.py:152
  (555 shorter events, 71.6 us)
Async XLA Ops:
  7.2 308.5 %all-reduce.6.cloned.1.call-start = ((), (), s32[]{:S(2)}) async-start(), calls=%async_computation | async-start | bytes 7077888 | tf_op jit(solution)/shard_map/psum | solution.py:146
  7.9 30.2 %copy-start.155 = (s32[2]{0:T(128)}, s32[2]{0:T(128)S(1)}, u32[]{:S(2)}) copy-start(s32[2]{0:T(128)S(1)} %get-tuple-element.9) | copy-start | bytes 28
  8.6 15.5 %copy-start.156 = (pred[2]{0:T(512)(128)(4,1)}, pred[2]{0:T(512)(128)(4,1)S(1)}, u32[]{:S(2)}) copy-start(pred[2]{0:T(512)(128)(4,1)S(1)} %broadcast_compare_fusion) | copy-start | bytes 10
  11.2 13.0 %collective-permute-start.8 = (bf16[1,16,8,128]{3,2,1,0:T(8,128)(2,1)S(1)}, bf16[1,16,8,128]{3,2,1,0:T(8,128)(2,1)S(1)}, u32[]{:S(2)}, u32[]{:S(2)}) collective-permute-start(bf16[1,16,8,128]{3,2,1,0:T(8,128)(2,1)S(1)} %get-tuple-element.24), channel_id=1, source_target_pairs={{0,8},{8,16},{16,24},{1,9},{9,17},{17,25},{2,10},{10,18},{18,26},{... | collective-permute-start | bytes 98312 | tf_op jit(solution)/shard_map/ppermute | solution.py:21
  16.1 8.1 %collective-permute-start.9 = (bf16[1,16,8,128]{3,2,1,0:T(8,128)(2,1)S(1)}, bf16[1,16,8,128]{3,2,1,0:T(8,128)(2,1)S(1)}, u32[]{:S(2)}, u32[]{:S(2)}) collective-permute-start(bf16[1,16,8,128]{3,2,1,0:T(8,128)(2,1)S(1)} %get-tuple-element.25), channel_id=1, source_target_pairs={{8,0},{16,8},{24,16},{9,1},{17,9},{25,17},{10,2},{18,10},{26,18},{... | collective-permute-start | bytes 98312 | tf_op jit(solution)/shard_map/ppermute | solution.py:23
  18.3 8.6 %collective-permute-start = (bf16[1,16,8,128]{3,2,1,0:T(8,128)(2,1)S(1)}, bf16[1,16,8,128]{3,2,1,0:T(8,128)(2,1)S(1)}, u32[]{:S(2)}, u32[]{:S(2)}) collective-permute-start(bf16[1,16,8,128]{3,2,1,0:T(8,128)(2,1)S(1)} %get-tuple-element.28), channel_id=1, source_target_pairs={{0,8},{8,16},{16,24},{1,9},{9,17},{17,25},{2,10},{10,18},{18,26},{... | collective-permute-start | bytes 98312 | tf_op jit(solution)/shard_map/ppermute | solution.py:21
  22.8 6.2 %collective-permute-start.1 = (bf16[1,16,8,128]{3,2,1,0:T(8,128)(2,1)S(1)}, bf16[1,16,8,128]{3,2,1,0:T(8,128)(2,1)S(1)}, u32[]{:S(2)}, u32[]{:S(2)}) collective-permute-start(bf16[1,16,8,128]{3,2,1,0:T(8,128)(2,1)S(1)} %get-tuple-element.29), channel_id=1, source_target_pairs={{8,0},{16,8},{24,16},{9,1},{17,9},{25,17},{10,2},{18,10},{26,18},{... | collective-permute-start | bytes 98312 | tf_op jit(solution)/shard_map/ppermute | solution.py:23
  24.2 8.8 %collective-permute-start.10 = (bf16[18,1,8,128]{3,2,1,0:T(8,128)(2,1)S(1)}, bf16[18,1,8,128]{3,2,1,0:T(8,128)(2,1)S(1)}, u32[]{:S(2)}, u32[]{:S(2)}) collective-permute-start(bf16[18,1,8,128]{3,2,1,0:T(8,128)(2,1)S(1)} %get-tuple-element.16), channel_id=1, source_target_pairs={{0,1},{1,2},{2,3},{3,4},{4,5},{5,6},{6,7},{8,9},{9,10},{10,11},{11... | collective-permute-start | bytes 110600 | tf_op jit(solution)/shard_map/ppermute | solution.py:21
  25.5 7.5 %collective-permute-start.11 = (bf16[18,1,8,128]{3,2,1,0:T(8,128)(2,1)S(1)}, bf16[18,1,8,128]{3,2,1,0:T(8,128)(2,1)S(1)}, u32[]{:S(2)}, u32[]{:S(2)}) collective-permute-start(bf16[18,1,8,128]{3,2,1,0:T(8,128)(2,1)S(1)} %get-tuple-element.17), channel_id=1, source_target_pairs={{1,0},{2,1},{3,2},{4,3},{5,4},{6,5},{7,6},{9,8},{10,9},{11,10},{12... | collective-permute-start | bytes 110600 | tf_op jit(solution)/shard_map/ppermute | solution.py:23
  29.0 8.9 %collective-permute-start.2 = (bf16[18,1,8,128]{3,2,1,0:T(8,128)(2,1)S(1)}, bf16[18,1,8,128]{3,2,1,0:T(8,128)(2,1)S(1)}, u32[]{:S(2)}, u32[]{:S(2)}) collective-permute-start(bf16[18,1,8,128]{3,2,1,0:T(8,128)(2,1)S(1)} %get-tuple-element.20), channel_id=1, source_target_pairs={{0,1},{1,2},{2,3},{3,4},{4,5},{5,6},{6,7},{8,9},{9,10},{10,11},{11... | collective-permute-start | bytes 110600 | tf_op jit(solution)/shard_map/ppermute | solution.py:21
  31.7 6.2 %collective-permute-start.3 = (bf16[18,1,8,128]{3,2,1,0:T(8,128)(2,1)S(1)}, bf16[18,1,8,128]{3,2,1,0:T(8,128)(2,1)S(1)}, u32[]{:S(2)}, u32[]{:S(2)}) collective-permute-start(bf16[18,1,8,128]{3,2,1,0:T(8,128)(2,1)S(1)} %get-tuple-element.21), channel_id=1, source_target_pairs={{1,0},{2,1},{3,2},{4,3},{5,4},{6,5},{7,6},{9,8},{10,9},{11,10},{12... | collective-permute-start | bytes 110600 | tf_op jit(solution)/shard_map/ppermute | solution.py:23
  39.1 4.6 %copy-start.17 = (bf16[2,8,8,8,128]{4,3,2,1,0:T(8,128)(2,1)}, bf16[2,8,8,8,128]{4,3,2,1,0:T(8,128)(2,1)S(1)}, u32[]{:S(2)}) copy-start(bf16[2,8,8,8,128]{4,3,2,1,0:T(8,128)(2,1)S(1)} %get-tuple-element.132) | copy-start | bytes 786436
  39.1 5.3 %copy-start.7 = (bf16[2,8,8,8,128]{4,3,2,1,0:T(8,128)(2,1)}, bf16[2,8,8,8,128]{4,3,2,1,0:T(8,128)(2,1)S(1)}, u32[]{:S(2)}) copy-start(bf16[2,8,8,8,128]{4,3,2,1,0:T(8,128)(2,1)S(1)} %get-tuple-element.131) | copy-start | bytes 786436
  40.3 4.6 %copy-start.19 = (bf16[2,8,8,8,128]{4,3,2,1,0:T(8,128)(2,1)}, bf16[2,8,8,8,128]{4,3,2,1,0:T(8,128)(2,1)S(1)}, u32[]{:S(2)}) copy-start(bf16[2,8,8,8,128]{4,3,2,1,0:T(8,128)(2,1)S(1)} %get-tuple-element.123) | copy-start | bytes 786436
  40.3 4.8 %copy-start.15 = (bf16[2,8,8,8,128]{4,3,2,1,0:T(8,128)(2,1)}, bf16[2,8,8,8,128]{4,3,2,1,0:T(8,128)(2,1)S(1)}, u32[]{:S(2)}) copy-start(bf16[2,8,8,8,128]{4,3,2,1,0:T(8,128)(2,1)S(1)} %get-tuple-element.129) | copy-start | bytes 786436
  40.4 5.0 %copy-start.13 = (bf16[2,8,8,8,128]{4,3,2,1,0:T(8,128)(2,1)}, bf16[2,8,8,8,128]{4,3,2,1,0:T(8,128)(2,1)S(1)}, u32[]{:S(2)}) copy-start(bf16[2,8,8,8,128]{4,3,2,1,0:T(8,128)(2,1)S(1)} %get-tuple-element.124) | copy-start | bytes 786436
  40.4 5.2 %copy-start.11 = (bf16[2,8,8,8,128]{4,3,2,1,0:T(8,128)(2,1)}, bf16[2,8,8,8,128]{4,3,2,1,0:T(8,128)(2,1)S(1)}, u32[]{:S(2)}) copy-start(bf16[2,8,8,8,128]{4,3,2,1,0:T(8,128)(2,1)S(1)} %get-tuple-element.125) | copy-start | bytes 786436
  40.4 5.4 %copy-start.9 = (bf16[2,8,8,8,128]{4,3,2,1,0:T(8,128)(2,1)}, bf16[2,8,8,8,128]{4,3,2,1,0:T(8,128)(2,1)S(1)}, u32[]{:S(2)}) copy-start(bf16[2,8,8,8,128]{4,3,2,1,0:T(8,128)(2,1)S(1)} %get-tuple-element.128) | copy-start | bytes 786436
  40.4 5.6 %copy-start.5 = (bf16[2,8,8,8,128]{4,3,2,1,0:T(8,128)(2,1)}, bf16[2,8,8,8,128]{4,3,2,1,0:T(8,128)(2,1)S(1)}, u32[]{:S(2)}) copy-start(bf16[2,8,8,8,128]{4,3,2,1,0:T(8,128)(2,1)S(1)} %get-tuple-element.126) | copy-start | bytes 786436
  40.4 5.9 %copy-start.3 = (bf16[2,8,8,8,128]{4,3,2,1,0:T(8,128)(2,1)}, bf16[2,8,8,8,128]{4,3,2,1,0:T(8,128)(2,1)S(1)}, u32[]{:S(2)}) copy-start(bf16[2,8,8,8,128]{4,3,2,1,0:T(8,128)(2,1)S(1)} %get-tuple-element.127) | copy-start | bytes 786436
  73.3 9.4 %copy-start.163 = (f32[128]{0:T(128)S(1)}, f32[128]{0:T(128)}, u32[]{:S(2)}) copy-start(f32[128]{0:T(128)} %get-tuple-element.4) | copy-start | bytes 1540
  75.6 52.2 %copy-start.100 = (bf16[2,8,8,8,128]{4,3,2,1,0:T(8,128)(2,1)S(1)}, bf16[2,8,8,8,128]{4,3,2,1,0:T(8,128)(2,1)}, u32[]{:S(2)}) copy-start(bf16[2,8,8,8,128]{4,3,2,1,0:T(8,128)(2,1)} %get-tuple-element.12) | copy-start | bytes 786436
  76.5 60.1 %collective-permute-start.4 = (bf16[1,16,8,128]{3,2,1,0:T(8,128)(2,1)S(1)}, bf16[1,16,8,128]{3,2,1,0:T(8,128)(2,1)S(1)}, u32[]{:S(2)}, u32[]{:S(2)}) collective-permute-start(bf16[1,16,8,128]{3,2,1,0:T(8,128)(2,1)S(1)} %get-tuple-element.26), channel_id=1, source_target_pairs={{0,8},{8,16},{16,24},{1,9},{9,17},{17,25},{2,10},{10,18},{18,26},{... | collective-permute-start | bytes 98312 | tf_op jit(solution)/shard_map/ppermute | solution.py:21
  81.4 55.2 %collective-permute-start.5 = (bf16[1,16,8,128]{3,2,1,0:T(8,128)(2,1)S(1)}, bf16[1,16,8,128]{3,2,1,0:T(8,128)(2,1)S(1)}, u32[]{:S(2)}, u32[]{:S(2)}) collective-permute-start(bf16[1,16,8,128]{3,2,1,0:T(8,128)(2,1)S(1)} %get-tuple-element.27), channel_id=1, source_target_pairs={{8,0},{16,8},{24,16},{9,1},{17,9},{25,17},{10,2},{18,10},{26,18},{... | collective-permute-start | bytes 98312 | tf_op jit(solution)/shard_map/ppermute | solution.py:23
  127.7 8.9 %copy-start.161 = (f32[128]{0:T(128)}, f32[128]{0:T(128)S(1)}, u32[]{:S(2)}) copy-start(f32[128]{0:T(128)S(1)} %psum.15) | copy-start | bytes 1540
  131.0 8.1 %collective-permute-start.12 = (bf16[1,16,8,128]{3,2,1,0:T(8,128)(2,1)S(1)}, bf16[1,16,8,128]{3,2,1,0:T(8,128)(2,1)S(1)}, u32[]{:S(2)}, u32[]{:S(2)}) collective-permute-start(bf16[1,16,8,128]{3,2,1,0:T(8,128)(2,1)S(1)} %get-tuple-element.22), channel_id=1, source_target_pairs={{0,8},{8,16},{16,24},{1,9},{9,17},{17,25},{2,10},{10,18},{18,26},{... | collective-permute-start | bytes 98312 | tf_op jit(solution)/shard_map/ppermute | solution.py:21
  135.2 5.8 %collective-permute-start.13 = (bf16[1,16,8,128]{3,2,1,0:T(8,128)(2,1)S(1)}, bf16[1,16,8,128]{3,2,1,0:T(8,128)(2,1)S(1)}, u32[]{:S(2)}, u32[]{:S(2)}) collective-permute-start(bf16[1,16,8,128]{3,2,1,0:T(8,128)(2,1)S(1)} %get-tuple-element.23), channel_id=1, source_target_pairs={{8,0},{16,8},{24,16},{9,1},{17,9},{25,17},{10,2},{18,10},{26,18},{... | collective-permute-start | bytes 98312 | tf_op jit(solution)/shard_map/ppermute | solution.py:23
  136.6 10.1 %collective-permute-start.6 = (bf16[18,1,8,128]{3,2,1,0:T(8,128)(2,1)S(1)}, bf16[18,1,8,128]{3,2,1,0:T(8,128)(2,1)S(1)}, u32[]{:S(2)}, u32[]{:S(2)}) collective-permute-start(bf16[18,1,8,128]{3,2,1,0:T(8,128)(2,1)S(1)} %get-tuple-element.18), channel_id=1, source_target_pairs={{0,1},{1,2},{2,3},{3,4},{4,5},{5,6},{6,7},{8,9},{9,10},{10,11},{11... | collective-permute-start | bytes 110600 | tf_op jit(solution)/shard_map/ppermute | solution.py:21
  137.9 8.8 %collective-permute-start.7 = (bf16[18,1,8,128]{3,2,1,0:T(8,128)(2,1)S(1)}, bf16[18,1,8,128]{3,2,1,0:T(8,128)(2,1)S(1)}, u32[]{:S(2)}, u32[]{:S(2)}) collective-permute-start(bf16[18,1,8,128]{3,2,1,0:T(8,128)(2,1)S(1)} %get-tuple-element.19), channel_id=1, source_target_pairs={{1,0},{2,1},{3,2},{4,3},{5,4},{6,5},{7,6},{9,8},{10,9},{11,10},{12... | collective-permute-start | bytes 110600 | tf_op jit(solution)/shard_map/ppermute | solution.py:23
  141.7 11.9 %collective-permute-start.14 = (bf16[18,1,8,128]{3,2,1,0:T(8,128)(2,1)}, bf16[18,1,8,128]{3,2,1,0:T(8,128)(2,1)}, u32[]{:S(2)}, u32[]{:S(2)}) collective-permute-start(bf16[18,1,8,128]{3,2,1,0:T(8,128)(2,1)} %get-tuple-element.14), channel_id=1, source_target_pairs={{0,1},{1,2},{2,3},{3,4},{4,5},{5,6},{6,7},{8,9},{9,10},{10,11},{11... | collective-permute-start | bytes 110600 | tf_op jit(solution)/shard_map/ppermute | solution.py:21
  145.2 8.4 %collective-permute-start.15 = (bf16[18,1,8,128]{3,2,1,0:T(8,128)(2,1)}, bf16[18,1,8,128]{3,2,1,0:T(8,128)(2,1)}, u32[]{:S(2)}, u32[]{:S(2)}) collective-permute-start(bf16[18,1,8,128]{3,2,1,0:T(8,128)(2,1)} %get-tuple-element.15), channel_id=1, source_target_pairs={{1,0},{2,1},{3,2},{4,3},{5,4},{6,5},{7,6},{9,8},{10,9},{11,10},{12... | collective-permute-start | bytes 110600 | tf_op jit(solution)/shard_map/ppermute | solution.py:23
  191.8 128.7 %copy-start.162 = (f32[128]{0:T(128)S(1)}, f32[128]{0:T(128)}, u32[]{:S(2)}) copy-start(f32[128]{0:T(128)} %copy-done.161) | copy-start | bytes 1540
  (149 other events, 231.9 us)
Sparse Core Ops, SparseCore 0:
  172.4 143.1 all-reduce.5
where the time goes:
time: 334 us; the launch traced here: 332 us
  waiting for transfers between devices  128 us (38%)
  blocking collectives  45 us (13%)
  matrix products  43.2 us (13%)
  starting transfers between devices  37.9 us (11%)
  local copies, waits for them, and re-layouts  33.8 us (10%)
  other arithmetic  25.6 us (8%)
  between operations  18.6 us (6%)
    psum x1, waiting for transfers between devices, per_device(): lax.psum((jnp.concatenate([first_grad, second_grad]), gain_grad), ('gx',...  124 us
    psum x1, blocking collectives, per_device(): lax.psum((jnp.concatenate([first_grad, second_grad]), gain_grad), ('gx',...  45 us
    ppermute x8, starting transfers between devices, with_halo(): lax.ppermute(tail, axis, [(i, (i + 1) % count) for i in range(ends)])  27.3 us
    dot_general x54, matrix products, tap_grads(): lax.dot_general(window, flat_rows, (((0,), (0,)), ((), ())), preferred_el...  15.4 us
    dot_general x54, matrix products, apply_taps(): lax.dot_general(window, kernel[tap_index], (((1,), (1,)), ((), ())), pref...  14.3 us
    slice x8, local copies, waits for them, and re-layouts, apply_taps(): tile_set[:, start_x:start_x + 8, start_y:start_y + 8, start_z:start_z + 8...  13.6 us
    dot_general x54, matrix products, apply_taps(): jnp.dot(window, kernel[tap_index], preferred_element_type=jnp.float32)  13.4 us
    ppermute x8, starting transfers between devices, with_halo(): lax.ppermute(head, axis, [((i + 1) % count, i) for i in range(ends)])  10.5 us
  transfers between devices with their start and end apart: 17, of which 3 were waited for; matrix products, arithmetic and copies ran while one was open for 9% of the time, Pallas kernels for 0%

commit v1 on v0

--- a/solution.py
+++ b/solution.py
@@ -144,7 +144,7 @@
         jnp.bfloat16
     )
     combined, gain_summed = lax.psum(
-        (jnp.concatenate([first_grad, second_grad]), gain_grad), ("gx", "gy")
+        lax.psum((jnp.concatenate([first_grad, second_grad]), gain_grad), "gy"), "gx"
     )
     shrink = clip_factor(
         jnp.sum(combined * combined) + jnp.sum(gain_summed * gain_summed), channels

time: 334 us -> 354 us (1.060)
  waiting for transfers between devices: 128 us -> 165 us
  blocking collectives: 45 us -> 28.7 us
    psum x1 -> x2, waiting for transfers between devices: 124 us -> 161 us  [the longest x1 90.5 us: per_device(): lax.psum(lax.psum((jnp.concatenate([first_grad, second_grad]), gain_grad)...]
    psum x1 -> x2, blocking collectives: 45 us -> 28.7 us  [the longest x1 17.7 us: per_device(): lax.psum((jnp.concatenate([first_grad, second_grad]), gain_grad), 'gy')]
    unnamed x328 -> x334, local copies, waits for them, and re-layouts: 10.5 us -> 9.86 us
  transfers between devices with their start and end apart: 17 -> 18, of which waited for: 3 -> 4; matrix products, arithmetic and copies ran while one was open for 9% -> 9% of each run, Pallas kernels for 0% -> 0%
where the time goes in v1:
time: 354 us; the launch traced here: 352 us
  waiting for transfers between devices  165 us (47%)
  matrix products  44.1 us (12%)
  starting transfers between devices  36 us (10%)
  local copies, waits for them, and re-layouts  35.6 us (10%)
  blocking collectives  28.7 us (8%)
  other arithmetic  23.9 us (7%)
  between operations  18.7 us (5%)
    psum x1, waiting for transfers between devices, per_device(): lax.psum(lax.psum((jnp.concatenate([first_grad, second_grad]), gain_grad)...  90.5 us
    psum x1, waiting for transfers between devices, per_device(): lax.psum((jnp.concatenate([first_grad, second_grad]), gain_grad), 'gy')  70.4 us
    ppermute x8, starting transfers between devices, with_halo(): lax.ppermute(tail, axis, [(i, (i + 1) % count) for i in range(ends)])  25.2 us
    psum x1, blocking collectives, per_device(): lax.psum((jnp.concatenate([first_grad, second_grad]), gain_grad), 'gy')  17.7 us
    dot_general x54, matrix products, tap_grads(): lax.dot_general(window, flat_rows, (((0,), (0,)), ((), ())), preferred_el...  15.4 us
    dot_general x54, matrix products, apply_taps(): jnp.dot(window, kernel[tap_index], preferred_element_type=jnp.float32)  14.4 us
    dot_general x54, matrix products, apply_taps(): lax.dot_general(window, kernel[tap_index], (((1,), (1,)), ((), ())), pref...  14.3 us
    slice x8, local copies, waits for them, and re-layouts, apply_taps(): tile_set[:, start_x:start_x + 8, start_y:start_y + 8, start_z:start_z + 8...  13.7 us
  transfers between devices with their start and end apart: 18, of which 4 were waited for; matrix products, arithmetic and copies ran while one was open for 9% of the time, Pallas kernels for 0%

profile of v1, /device:TPU:0, one launch (start us, length us, event | category | flops | bytes accessed | tf_op | source)
XLA Modules:
  0.0 352.0 jit_solution(16772888888324633538)
XLA Ops:
  11.2 4.9 %collective-permute-start.8 = (bf16[1,16,8,128]{3,2,1,0:T(8,128)(2,1)S(1)}, bf16[1,16,8,128]{3,2,1,0:T(8,128)(2,1)S(1)}, u32[]{:S(2)}, u32[]{:S(2)}) collective-permute-start(bf16[1,16,8,128]{3,2,1,0:T(8,128)(2,1)S(1)} %get-tuple-element.24), channel_id=1, source_target_pairs={{0,8},{8,16},{16,24},{1,9},{9,17},{17,25},{2,10},{10,18},{18,26},{... | collective-permute-start | bytes 98312 | tf_op jit(solution)/shard_map/ppermute | solution.py:21
  16.1 1.3 collective-permute-start.9
  18.3 4.5 %collective-permute-start = (bf16[1,16,8,128]{3,2,1,0:T(8,128)(2,1)S(1)}, bf16[1,16,8,128]{3,2,1,0:T(8,128)(2,1)S(1)}, u32[]{:S(2)}, u32[]{:S(2)}) collective-permute-start(bf16[1,16,8,128]{3,2,1,0:T(8,128)(2,1)S(1)} %get-tuple-element.28), channel_id=1, source_target_pairs={{0,8},{8,16},{16,24},{1,9},{9,17},{17,25},{2,10},{10,18},{18,26},{... | collective-permute-start | bytes 98312 | tf_op jit(solution)/shard_map/ppermute | solution.py:21
  26.9 2.1 collective-permute-done.1
  29.0 2.7 collective-permute-start.2
  33.9 2.8 pad_slice_fusion.18
  36.6 1.4 fusion.300
  56.2 2.5 multiply_reduce_fusion.1
  59.4 2.9 fusion.293
  62.5 1.5 select_convert_fusion
  74.2 1.7 fusion.62
  76.8 4.9 %collective-permute-start.4 = (bf16[1,16,8,128]{3,2,1,0:T(8,128)(2,1)S(1)}, bf16[1,16,8,128]{3,2,1,0:T(8,128)(2,1)S(1)}, u32[]{:S(2)}, u32[]{:S(2)}) collective-permute-start(bf16[1,16,8,128]{3,2,1,0:T(8,128)(2,1)S(1)} %get-tuple-element.26), channel_id=1, source_target_pairs={{0,8},{8,16},{16,24},{1,9},{9,17},{17,25},{2,10},{10,18},{18,26},{... | collective-permute-start | bytes 98312 | tf_op jit(solution)/shard_map/ppermute | solution.py:21
  83.1 17.7 %psum.30 = f32[128]{0:T(128)S(1)} all-reduce(f32[128]{0:T(128)S(1)} %copy-done.166), channel_id=1, replica_groups=mesh['gx'=4,'gy'=8] {'gy'}, use_global_device_ids=true, to_apply=%region_12.13 | all-reduce | flops 128 | bytes 1024 | tf_op jit(solution)/shard_map/psum | solution.py:147
  100.7 11.0 %psum.31 = f32[128]{0:T(128)S(1)} all-reduce(f32[128]{0:T(128)S(1)} %psum.30), channel_id=1, replica_groups=mesh['gx'=4,'gy'=8] {'gx'}, use_global_device_ids=true, to_apply=%region_13.14 | all-reduce | flops 128 | bytes 1024 | tf_op jit(solution)/shard_map/psum | solution.py:146
  112.7 2.2 scatter_fusion.3
  116.6 3.6 %collective-permute-start.12 = (bf16[1,16,8,128]{3,2,1,0:T(8,128)(2,1)S(1)}, bf16[1,16,8,128]{3,2,1,0:T(8,128)(2,1)S(1)}, u32[]{:S(2)}, u32[]{:S(2)}) collective-permute-start(bf16[1,16,8,128]{3,2,1,0:T(8,128)(2,1)S(1)} %get-tuple-element.22), channel_id=1, source_target_pairs={{0,8},{8,16},{16,24},{1,9},{9,17},{17,25},{2,10},{10,18},{18,26},{... | collective-permute-start | bytes 98312 | tf_op jit(solution)/shard_map/ppermute | solution.py:21
  124.2 1.8 collective-permute-done.13
  126.7 1.9 collective-permute-start.14
  128.6 1.5 collective-permute-start.15
  131.1 1.8 gather_fusion.1
  132.9 2.6 pad_slice_fusion.36
  135.5 1.3 fusion.301
  136.9 1.8 pad_maximum_fusion.4
  138.6 1.8 gather_fusion.3
  140.5 2.7 pad_slice_fusion
  143.2 1.4 fusion.299
  153.5 2.0 pad_maximum_fusion
  155.9 1.4 convolution_add_fusion.77
  170.5 70.4 %all-reduce.7.cloned.1.call-done = f32[884736]{0:T(1024)} async-done(((f32[884736]{0:T(1024)}), f32[884736]{0:T(1024)}) %all-reduce.7.cloned.1.call-update) | async-done | bytes 3538960 | tf_op jit(solution)/shard_map/psum | solution.py:147
  247.1 90.5 %all-reduce.9.cloned.1.call-done = f32[884736]{0:T(1024)} async-done(((f32[884736]{0:T(1024)}), f32[884736]{0:T(1024)}) %all-reduce.9.cloned.1.call-update) | async-done | bytes 3538960 | tf_op jit(solution)/shard_map/psum | solution.py:146
  337.6 3.7 %multiply_reduce_fusion = f32[]{:T(128)} fusion(f32[884736]{0:T(1024)} %all-reduce.9.cloned.1.call-done), kind=kLoop, calls=%fused_computation.9 | loop fusion | flops 1769471 | bytes 3538948 | tf_op jit(solution)/shard_map/reduce_sum | solution.py:150
  343.1 2.0 broadcast_multiply_fusion
  (565 shorter events, 76.9 us)
Async XLA Ops:
  7.2 233.7 %all-reduce.7.cloned.1.call-start = ((), (), s32[]{:S(2)}) async-start(), calls=%async_computation | async-start | bytes 7077888 | tf_op jit(solution)/shard_map/psum | solution.py:147
  7.9 30.3 %copy-start.152 = (s32[2]{0:T(128)}, s32[2]{0:T(128)S(1)}, u32[]{:S(2)}) copy-start(s32[2]{0:T(128)S(1)} %get-tuple-element.9) | copy-start | bytes 28
  8.6 15.6 %copy-start.159 = (pred[2]{0:T(512)(128)(4,1)}, pred[2]{0:T(512)(128)(4,1)S(1)}, u32[]{:S(2)}) copy-start(pred[2]{0:T(512)(128)(4,1)S(1)} %broadcast_compare_fusion) | copy-start | bytes 10
  9.2 8.3 %copy-start.153 = (s32[2]{0:T(128)}, s32[2]{0:T(128)S(1)}, u32[]{:S(2)}) copy-start(s32[2]{0:T(128)S(1)} %fusion.291) | copy-start | bytes 28
  11.2 13.0 %collective-permute-start.8 = (bf16[1,16,8,128]{3,2,1,0:T(8,128)(2,1)S(1)}, bf16[1,16,8,128]{3,2,1,0:T(8,128)(2,1)S(1)}, u32[]{:S(2)}, u32[]{:S(2)}) collective-permute-start(bf16[1,16,8,128]{3,2,1,0:T(8,128)(2,1)S(1)} %get-tuple-element.24), channel_id=1, source_target_pairs={{0,8},{8,16},{16,24},{1,9},{9,17},{17,25},{2,10},{10,18},{18,26},{... | collective-permute-start | bytes 98312 | tf_op jit(solution)/shard_map/ppermute | solution.py:21
  16.1 8.1 %collective-permute-start.9 = (bf16[1,16,8,128]{3,2,1,0:T(8,128)(2,1)S(1)}, bf16[1,16,8,128]{3,2,1,0:T(8,128)(2,1)S(1)}, u32[]{:S(2)}, u32[]{:S(2)}) collective-permute-start(bf16[1,16,8,128]{3,2,1,0:T(8,128)(2,1)S(1)} %get-tuple-element.25), channel_id=1, source_target_pairs={{8,0},{16,8},{24,16},{9,1},{17,9},{25,17},{10,2},{18,10},{26,18},{... | collective-permute-start | bytes 98312 | tf_op jit(solution)/shard_map/ppermute | solution.py:23
  18.3 8.6 %collective-permute-start = (bf16[1,16,8,128]{3,2,1,0:T(8,128)(2,1)S(1)}, bf16[1,16,8,128]{3,2,1,0:T(8,128)(2,1)S(1)}, u32[]{:S(2)}, u32[]{:S(2)}) collective-permute-start(bf16[1,16,8,128]{3,2,1,0:T(8,128)(2,1)S(1)} %get-tuple-element.28), channel_id=1, source_target_pairs={{0,8},{8,16},{16,24},{1,9},{9,17},{17,25},{2,10},{10,18},{18,26},{... | collective-permute-start | bytes 98312 | tf_op jit(solution)/shard_map/ppermute | solution.py:21
  22.8 6.2 %collective-permute-start.1 = (bf16[1,16,8,128]{3,2,1,0:T(8,128)(2,1)S(1)}, bf16[1,16,8,128]{3,2,1,0:T(8,128)(2,1)S(1)}, u32[]{:S(2)}, u32[]{:S(2)}) collective-permute-start(bf16[1,16,8,128]{3,2,1,0:T(8,128)(2,1)S(1)} %get-tuple-element.29), channel_id=1, source_target_pairs={{8,0},{16,8},{24,16},{9,1},{17,9},{25,17},{10,2},{18,10},{26,18},{... | collective-permute-start | bytes 98312 | tf_op jit(solution)/shard_map/ppermute | solution.py:23
  24.2 31.9 %copy-start.156 = (pred[1024]{0:T(1024)(128)(4,1)}, pred[1024]{0:T(1024)(128)(4,1)S(1)}, u32[]{:S(2)}) copy-start(pred[1024]{0:T(1024)(128)(4,1)S(1)} %broadcast_in_dim.109) | copy-start | bytes 3076
  24.3 8.8 %collective-permute-start.10 = (bf16[18,1,8,128]{3,2,1,0:T(8,128)(2,1)S(1)}, bf16[18,1,8,128]{3,2,1,0:T(8,128)(2,1)S(1)}, u32[]{:S(2)}, u32[]{:S(2)}) collective-permute-start(bf16[18,1,8,128]{3,2,1,0:T(8,128)(2,1)S(1)} %get-tuple-element.16), channel_id=1, source_target_pairs={{0,1},{1,2},{2,3},{3,4},{4,5},{5,6},{6,7},{8,9},{9,10},{10,11},{11... | collective-permute-start | bytes 110600 | tf_op jit(solution)/shard_map/ppermute | solution.py:21
  25.6 7.5 %collective-permute-start.11 = (bf16[18,1,8,128]{3,2,1,0:T(8,128)(2,1)S(1)}, bf16[18,1,8,128]{3,2,1,0:T(8,128)(2,1)S(1)}, u32[]{:S(2)}, u32[]{:S(2)}) collective-permute-start(bf16[18,1,8,128]{3,2,1,0:T(8,128)(2,1)S(1)} %get-tuple-element.17), channel_id=1, source_target_pairs={{1,0},{2,1},{3,2},{4,3},{5,4},{6,5},{7,6},{9,8},{10,9},{11,10},{12... | collective-permute-start | bytes 110600 | tf_op jit(solution)/shard_map/ppermute | solution.py:23
  29.0 9.0 %collective-permute-start.2 = (bf16[18,1,8,128]{3,2,1,0:T(8,128)(2,1)S(1)}, bf16[18,1,8,128]{3,2,1,0:T(8,128)(2,1)S(1)}, u32[]{:S(2)}, u32[]{:S(2)}) collective-permute-start(bf16[18,1,8,128]{3,2,1,0:T(8,128)(2,1)S(1)} %get-tuple-element.20), channel_id=1, source_target_pairs={{0,1},{1,2},{2,3},{3,4},{4,5},{5,6},{6,7},{8,9},{9,10},{10,11},{11... | collective-permute-start | bytes 110600 | tf_op jit(solution)/shard_map/ppermute | solution.py:21
  31.8 6.3 %collective-permute-start.3 = (bf16[18,1,8,128]{3,2,1,0:T(8,128)(2,1)S(1)}, bf16[18,1,8,128]{3,2,1,0:T(8,128)(2,1)S(1)}, u32[]{:S(2)}, u32[]{:S(2)}) collective-permute-start(bf16[18,1,8,128]{3,2,1,0:T(8,128)(2,1)S(1)} %get-tuple-element.21), channel_id=1, source_target_pairs={{1,0},{2,1},{3,2},{4,3},{5,4},{6,5},{7,6},{9,8},{10,9},{11,10},{12... | collective-permute-start | bytes 110600 | tf_op jit(solution)/shard_map/ppermute | solution.py:23
  39.2 5.3 %copy-start.7 = (bf16[2,8,8,8,128]{4,3,2,1,0:T(8,128)(2,1)}, bf16[2,8,8,8,128]{4,3,2,1,0:T(8,128)(2,1)S(1)}, u32[]{:S(2)}) copy-start(bf16[2,8,8,8,128]{4,3,2,1,0:T(8,128)(2,1)S(1)} %get-tuple-element.131) | copy-start | bytes 786436
  40.6 5.1 %copy-start.11 = (bf16[2,8,8,8,128]{4,3,2,1,0:T(8,128)(2,1)}, bf16[2,8,8,8,128]{4,3,2,1,0:T(8,128)(2,1)S(1)}, u32[]{:S(2)}) copy-start(bf16[2,8,8,8,128]{4,3,2,1,0:T(8,128)(2,1)S(1)} %get-tuple-element.125) | copy-start | bytes 786436
  40.6 5.3 %copy-start.9 = (bf16[2,8,8,8,128]{4,3,2,1,0:T(8,128)(2,1)}, bf16[2,8,8,8,128]{4,3,2,1,0:T(8,128)(2,1)S(1)}, u32[]{:S(2)}) copy-start(bf16[2,8,8,8,128]{4,3,2,1,0:T(8,128)(2,1)S(1)} %get-tuple-element.128) | copy-start | bytes 786436
  40.6 5.5 %copy-start.5 = (bf16[2,8,8,8,128]{4,3,2,1,0:T(8,128)(2,1)}, bf16[2,8,8,8,128]{4,3,2,1,0:T(8,128)(2,1)S(1)}, u32[]{:S(2)}) copy-start(bf16[2,8,8,8,128]{4,3,2,1,0:T(8,128)(2,1)S(1)} %get-tuple-element.126) | copy-start | bytes 786436
  40.6 5.7 %copy-start.3 = (bf16[2,8,8,8,128]{4,3,2,1,0:T(8,128)(2,1)}, bf16[2,8,8,8,128]{4,3,2,1,0:T(8,128)(2,1)S(1)}, u32[]{:S(2)}) copy-start(bf16[2,8,8,8,128]{4,3,2,1,0:T(8,128)(2,1)S(1)} %get-tuple-element.127) | copy-start | bytes 786436
  74.2 8.8 %copy-start.166 = (f32[128]{0:T(128)S(1)}, f32[128]{0:T(128)}, u32[]{:S(2)}) copy-start(f32[128]{0:T(128)} %get-tuple-element.4) | copy-start | bytes 1540
  75.9 36.7 %copy-start.155 = (s32[2]{0:T(128)S(1)}, s32[2]{0:T(128)}, u32[]{:S(2)}) copy-start(s32[2]{0:T(128)} %copy-done.153) | copy-start | bytes 28
  76.8 44.7 %collective-permute-start.4 = (bf16[1,16,8,128]{3,2,1,0:T(8,128)(2,1)S(1)}, bf16[1,16,8,128]{3,2,1,0:T(8,128)(2,1)S(1)}, u32[]{:S(2)}, u32[]{:S(2)}) collective-permute-start(bf16[1,16,8,128]{3,2,1,0:T(8,128)(2,1)S(1)} %get-tuple-element.26), channel_id=1, source_target_pairs={{0,8},{8,16},{16,24},{1,9},{9,17},{17,25},{2,10},{10,18},{18,26},{... | collective-permute-start | bytes 98312 | tf_op jit(solution)/shard_map/ppermute | solution.py:21
  81.7 39.8 %collective-permute-start.5 = (bf16[1,16,8,128]{3,2,1,0:T(8,128)(2,1)S(1)}, bf16[1,16,8,128]{3,2,1,0:T(8,128)(2,1)S(1)}, u32[]{:S(2)}, u32[]{:S(2)}) collective-permute-start(bf16[1,16,8,128]{3,2,1,0:T(8,128)(2,1)S(1)} %get-tuple-element.27), channel_id=1, source_target_pairs={{8,0},{16,8},{24,16},{9,1},{17,9},{25,17},{10,2},{18,10},{26,18},{... | collective-permute-start | bytes 98312 | tf_op jit(solution)/shard_map/ppermute | solution.py:23
  111.7 9.8 %copy-start.164 = (f32[128]{0:T(128)}, f32[128]{0:T(128)S(1)}, u32[]{:S(2)}) copy-start(f32[128]{0:T(128)S(1)} %psum.31) | copy-start | bytes 1540
  116.6 7.6 %collective-permute-start.12 = (bf16[1,16,8,128]{3,2,1,0:T(8,128)(2,1)S(1)}, bf16[1,16,8,128]{3,2,1,0:T(8,128)(2,1)S(1)}, u32[]{:S(2)}, u32[]{:S(2)}) collective-permute-start(bf16[1,16,8,128]{3,2,1,0:T(8,128)(2,1)S(1)} %get-tuple-element.22), channel_id=1, source_target_pairs={{0,8},{8,16},{16,24},{1,9},{9,17},{17,25},{2,10},{10,18},{18,26},{... | collective-permute-start | bytes 98312 | tf_op jit(solution)/shard_map/ppermute | solution.py:21
  120.2 5.8 %collective-permute-start.13 = (bf16[1,16,8,128]{3,2,1,0:T(8,128)(2,1)S(1)}, bf16[1,16,8,128]{3,2,1,0:T(8,128)(2,1)S(1)}, u32[]{:S(2)}, u32[]{:S(2)}) collective-permute-start(bf16[1,16,8,128]{3,2,1,0:T(8,128)(2,1)S(1)} %get-tuple-element.23), channel_id=1, source_target_pairs={{8,0},{16,8},{24,16},{9,1},{17,9},{25,17},{10,2},{18,10},{26,18},{... | collective-permute-start | bytes 98312 | tf_op jit(solution)/shard_map/ppermute | solution.py:23
  121.6 8.5 %collective-permute-start.6 = (bf16[18,1,8,128]{3,2,1,0:T(8,128)(2,1)S(1)}, bf16[18,1,8,128]{3,2,1,0:T(8,128)(2,1)S(1)}, u32[]{:S(2)}, u32[]{:S(2)}) collective-permute-start(bf16[18,1,8,128]{3,2,1,0:T(8,128)(2,1)S(1)} %get-tuple-element.18), channel_id=1, source_target_pairs={{0,1},{1,2},{2,3},{3,4},{4,5},{5,6},{6,7},{8,9},{9,10},{10,11},{11... | collective-permute-start | bytes 110600 | tf_op jit(solution)/shard_map/ppermute | solution.py:21
  122.9 7.2 %collective-permute-start.7 = (bf16[18,1,8,128]{3,2,1,0:T(8,128)(2,1)S(1)}, bf16[18,1,8,128]{3,2,1,0:T(8,128)(2,1)S(1)}, u32[]{:S(2)}, u32[]{:S(2)}) collective-permute-start(bf16[18,1,8,128]{3,2,1,0:T(8,128)(2,1)S(1)} %get-tuple-element.19), channel_id=1, source_target_pairs={{1,0},{2,1},{3,2},{4,3},{5,4},{6,5},{7,6},{9,8},{10,9},{11,10},{12... | collective-permute-start | bytes 110600 | tf_op jit(solution)/shard_map/ppermute | solution.py:23
  126.7 10.2 %collective-permute-start.14 = (bf16[18,1,8,128]{3,2,1,0:T(8,128)(2,1)}, bf16[18,1,8,128]{3,2,1,0:T(8,128)(2,1)}, u32[]{:S(2)}, u32[]{:S(2)}) collective-permute-start(bf16[18,1,8,128]{3,2,1,0:T(8,128)(2,1)} %get-tuple-element.14), channel_id=1, source_target_pairs={{0,1},{1,2},{2,3},{3,4},{4,5},{5,6},{6,7},{8,9},{9,10},{10,11},{11... | collective-permute-start | bytes 110600 | tf_op jit(solution)/shard_map/ppermute | solution.py:21
  128.6 8.3 %collective-permute-start.15 = (bf16[18,1,8,128]{3,2,1,0:T(8,128)(2,1)}, bf16[18,1,8,128]{3,2,1,0:T(8,128)(2,1)}, u32[]{:S(2)}, u32[]{:S(2)}) collective-permute-start(bf16[18,1,8,128]{3,2,1,0:T(8,128)(2,1)} %get-tuple-element.15), channel_id=1, source_target_pairs={{1,0},{2,1},{3,2},{4,3},{5,4},{6,5},{7,6},{9,8},{10,9},{11,10},{12... | collective-permute-start | bytes 110600 | tf_op jit(solution)/shard_map/ppermute | solution.py:23
  155.6 182.0 %all-reduce.9.cloned.1.call-start = ((), (), s32[]{:S(2)}) async-start(), calls=%async_computation.1 | async-start | bytes 7077888 | tf_op jit(solution)/shard_map/psum | solution.py:146
  247.1 95.5 %copy-start.165 = (f32[128]{0:T(128)S(1)}, f32[128]{0:T(128)}, u32[]{:S(2)}) copy-start(f32[128]{0:T(128)} %copy-done.164) | copy-start | bytes 1540
  337.6 5.5 %copy-start = (f32[884736]{0:T(1024)S(1)}, f32[884736]{0:T(1024)}, u32[]{:S(2)}) copy-start(f32[884736]{0:T(1024)} %all-reduce.9.cloned.1.call-done) | copy-start | bytes 10616836
  (153 other events, 258.7 us)
Sparse Core Ops, SparseCore 0:
  155.7 85.1 all-reduce.6
  244.0 93.5 all-reduce.8
